TPU v7x, 32 devices: a whole 2x2x4 slice. The times are simulated.
32 devices in a mesh: shard: 2 (over y), blk: 4 (over z), ckpt: 2 (over x), qry: 2 (over core).
Axes of the slice: x: 2, y: 2, z: 4, core: 2. Of those that a mesh axis runs over, the one named last changes fastest.
Arguments:
- query_feats: bfloat16 [2, 8192, 2048], P('ckpt', ('shard', 'blk', 'qry')), parts along dimension 1, may hold values from -6 to 6
- train_feats: bfloat16 [2, 1024, 2048], P('ckpt', ('shard', 'blk')), parts along dimension 1, may hold values from -0.125 to 0.125
- loss_weights: bfloat16 [2, 1024], P('ckpt', ('shard', 'blk')), parts along dimension 1, may hold values from 0.099609375 to 1
- pair_list: int32 [32, 2], P(('shard', 'blk', 'qry')), parts along dimension 0, may hold values from 0 to 3, all different within a row
- tile_owner: int32 [8], P('shard'), parts along dimension 0, may hold values from 0 to 3, each once
Outputs:
- scores: float32 [8192, 512], P(('shard', 'blk', 'qry'), 'ckpt'), parts along dimension 0
There are 2 independent parts, one for each index of `shard`. A program takes and returns all parts, laid end to end along the dimension named above; each array names one. Nothing has to cross between parts.
Inputs may be any that keep to these rules, and one draw needn't show every extreme that they name: `pair_list`: each row names 2 different training blocks; every training block is named by some row. `tile_owner`: a permutation of the training blocks.
All inputs are finite; a program needn't handle non-finite values.
Results may differ from a plain program's by a relative error of at most 0.0003.
Values may be sent and summed in bfloat16 or wider, within the bound.
No kernel may reach another device: no remote copies, remote signals or barrier semaphores. Data moves between devices by JAX's collectives and lax.ppermute only.
A program may use at most 128 MiB of HBM per device.

v0:
```python
import jax
import jax.numpy as jnp
from jax import lax
from jax.sharding import PartitionSpec as P

QBLK = 256
TBLK = 128


def per_device(query_feats, train_feats, loss_weights, pair_list, tile_owner):
    queries = query_feats[0]
    block_count = lax.axis_size("blk")
    total_rows = TBLK * block_count
    block_ids = jnp.arange(block_count, dtype=jnp.int32)
    wanted = jnp.any(pair_list[:, :, None] == block_ids[None, None, :], axis=1).astype(jnp.float32)
    own_rows = train_feats[0]
    own_weights = loss_weights[0]
    gathered_rows, gathered_weights = (
        lax.all_gather(own_rows, "blk", axis=0, tiled=True),
        lax.all_gather(own_weights, "blk", axis=0, tiled=True),
    )
    row_blocks = gathered_rows.reshape(block_count, TBLK, gathered_rows.shape[1])
    weight_blocks = gathered_weights.reshape(block_count, TBLK)
    query_mask = jnp.transpose(jnp.repeat(wanted, QBLK, axis=0))
    owner_rows = total_rows // lax.axis_size("ckpt")
    picked = row_blocks[tile_owner].reshape(lax.axis_size("ckpt") * owner_rows, row_blocks.shape[2])
    picked_weights = (
        weight_blocks[tile_owner].reshape(lax.axis_size("ckpt") * owner_rows).astype(jnp.float32)
    )
    products = lax.dot_general(
        picked, queries, (((1,), (1,)), ((), ())), preferred_element_type=jnp.float32
    )
    mask_rows = jnp.repeat(query_mask[tile_owner], TBLK, axis=0)
    summed_rows = lax.psum_scatter(
        products * picked_weights[:, None] * mask_rows, "ckpt", scatter_dimension=0, tiled=True
    )
    return jnp.transpose(summed_rows)


def solution(mesh):
    return jax.shard_map(
        per_device,
        mesh=mesh,
        in_specs=(
            P("ckpt", ("shard", "blk", "qry"), None),
            P("ckpt", ("shard", "blk"), None),
            P("ckpt", ("shard", "blk")),
            P(("shard", "blk", "qry"), None),
            P("shard"),
        ),
        out_specs=P(("shard", "blk", "qry"), "ckpt"),
        check_vma=False,
    )
```

profile of v0, /device:TPU:0, one launch (start us, length us, event | category | flops | bytes accessed | tf_op | source)
XLA Modules:
  0.0 93.2 jit_solution(14550216381288683997)
XLA Ops:
  6.5 0.0 copy-start
  6.5 0.0 all-gather.4.cloned.1.call-start
  6.5 0.7 all-gather.4.cloned.1.call-update
  7.3 0.0 reduce-scatter.2.cloned.1.call-start
  7.3 0.8 compare_reduce_fusion
  8.1 0.1 copy.7
  8.2 0.1 broadcast_bitcast_fusion
  8.3 0.7 compare_select_fusion
  8.9 0.6 gather_fusion.2
  9.5 12.8 %all-gather.1 = bf16[1,512]{1,0:T(2,128)(2,1)S(1)} all-gather(bf16[1,128]{1,0:T(2,128)(2,1)} %param.7), channel_id=3, replica_groups=mesh['shard'=2,'blk'=4,'ckpt'=2,'qry'=2] {'blk'}, dimensions={1}, use_global_device_ids=true | all-gather | bytes 1280 | tf_op jit(solution)/shard_map/all_gather | solution.py:20
  22.3 0.6 gather_fusion.1
  22.9 34.4 %all-gather.4.cloned.1.call-done = bf16[1,512,2048]{2,1,0:T(8,128)(2,1)} async-done(((bf16[1,128,2048]{2,1,0:T(8,128)(2,1)}), bf16[1,512,2048]{2,1,0:T(8,128)(2,1)}) %all-gather.4.cloned.1.call-update) | async-done | bytes 2097168 | tf_op jit(solution)/shard_map/all_gather | solution.py:19
  57.3 3.6 %gather_fusion = bf16[4,128,2048]{2,1,0:T(8,128)(2,1)} fusion(bf16[4,128,2048]{2,1,0:T(8,128)(2,1)} %bitcast.23, s32[1024]{0:T(1024)S(1)} %pad_clamp_fusion), kind=kCustom, calls=%fused_computation | custom fusion | bytes 4194320 | tf_op jit(solution)/shard_map/gather | solution.py:26
  60.9 0.1 broadcast_in_dim.16
  61.1 0.0 copy-done
  61.1 3.9 %fusion.5 = f32[512,512]{1,0:T(8,128)} fusion(f32[512,512]{1,0:T(8,128)S(1)} %bitcast.25, bf16[512,2048]{1,0:T(8,128)(2,1)} %bitcast.24, bf16[1,512,2048]{2,1,0:T(8,128)(2,1)S(1)} %copy-done, f32[512]{0:T(512)S(1)} %bitcast_convert_fusion), kind=kOutput, calls=%fused_computation.6 | convolution fusion | flops 1074266112 | bytes 6293504 | tf_op jit(solution)/shard_map/dot_general | solution.py:30
  64.9 0.0 reduce-scatter.2.cloned.1.call-update
  65.0 19.3 %reduce-scatter.2.cloned.1.call-done = f32[256,512]{1,0:T(8,128)} async-done(((f32[512,512]{1,0:T(8,128)}), f32[256,512]{1,0:T(8,128)}) %reduce-scatter.2.cloned.1.call-update) | async-done | bytes 524304 | tf_op jit(solution)/shard_map/reduce_scatter | solution.py:34
  84.3 2.0 %copy.8 = f32[512,256]{1,0:T(8,128)} copy(f32[512,256]{0,1:T(8,128)} %bitcast.27) | data formatting | bytes 1048576 | tf_op jit(solution)/shard_map/transpose | solution.py:37
  (5 shorter events, 0.0 us)
Async XLA Ops:
  6.5 54.5 %copy-start = (bf16[1,512,2048]{2,1,0:T(8,128)(2,1)S(1)}, bf16[1,512,2048]{2,1,0:T(8,128)(2,1)}, u32[]{:S(2)}) copy-start(bf16[1,512,2048]{2,1,0:T(8,128)(2,1)} %param.5) | copy-start | bytes 6291460
  6.5 50.8 %all-gather.4.cloned.1.call-start = ((), (), s32[]{:S(2)}) async-start(), calls=%async_computation.2 | async-start | bytes 2621440 | tf_op jit(solution)/shard_map/all_gather | solution.py:19
  7.3 77.0 %reduce-scatter.2.cloned.1.call-start = ((), (), s32[]{:S(2)}) async-start(), calls=%async_computation.1 | async-start | bytes 1572864 | tf_op jit(solution)/shard_map/reduce_scatter | solution.py:34
Sparse Core Ops, SparseCore 0:
  8.9 48.3 all-gather.3
  65.1 19.1 reduce-scatter.1
where the time goes:
time: 93.4 us; the launch traced here: 93.2 us
  waiting for transfers between devices  54.5 us (58%)
  between operations  13.4 us (14%)
  blocking collectives  12.8 us (14%)
  local copies, waits for them, and re-layouts  7.07 us (8%)
  matrix products  3.86 us (4%)
  other arithmetic  1.47 us (2%)
    all_gather x1, waiting for transfers between devices, per_device(): lax.all_gather(own_rows, 'blk', axis=0, tiled=True)  34.4 us
    reduce_scatter x1, waiting for transfers between devices, per_device(): lax.psum_scatter(products * picked_weights[:, None] * mask_rows, 'ckpt',...  19.3 us
    all_gather x1, blocking collectives, per_device(): lax.all_gather(own_weights, 'blk', axis=0, tiled=True)  12.8 us
    dot_general x1, matrix products, per_device(): lax.dot_general(picked, queries, (((1,), (1,)), ((), ())), preferred_elem...  3.86 us
    gather x1, local copies, waits for them, and re-layouts, per_device(): row_blocks[tile_owner]  3.62 us
    transpose x1, local copies, waits for them, and re-layouts, per_device(): return jnp.transpose(summed_rows)  2.04 us
  transfers between devices with their start and end apart: 2, of which 2 were waited for; matrix products, arithmetic and copies ran while one was open for 3% of the time, Pallas kernels for 0%

commit v1 on v0

--- a/solution.py
+++ b/solution.py
@@ -1,3 +1,4 @@
+import functools
 import jax
 import jax.numpy as jnp
 from jax import lax
@@ -5,6 +6,27 @@
 
 QBLK = 256
 TBLK = 128
+
+
+def chains_change(work_x, ax_name, d_out):
+    nodes = lax.axis_size(ax_name)
+    block_list = [work_x]
+    for i0 in range(1, nodes):
+        block_list.append(
+            lax.ppermute(
+                block_list[i0 - 1],
+                ax_name,
+                perm=[(hop_no, (hop_no - 1) % nodes) for hop_no in range(nodes)],
+            )
+        )
+    return jnp.roll(
+        jnp.concatenate(block_list, axis=d_out),
+        lax.axis_index(ax_name) * work_x.shape[d_out],
+        axis=d_out,
+    )
+
+
+_convert_indices = functools.partial(chains_change, ax_name="blk", d_out=0)
 
 
 def per_device(query_feats, train_feats, loss_weights, pair_list, tile_owner):
@@ -16,7 +38,7 @@
     own_rows = train_feats[0]
     own_weights = loss_weights[0]
     gathered_rows, gathered_weights = (
-        lax.all_gather(own_rows, "blk", axis=0, tiled=True),
+        _convert_indices(own_rows),
         lax.all_gather(own_weights, "blk", axis=0, tiled=True),
     )
     row_blocks = gathered_rows.reshape(block_count, TBLK, gathered_rows.shape[1])

time: 93.4 us -> 105 us (1.12)
  waiting for transfers between devices: 54.5 us -> 38.2 us
  local copies, waits for them, and re-layouts: 7.07 us -> 22.3 us
  starting transfers between devices: 0.04 us -> 9.26 us
  blocking collectives: 12.8 us -> 16.3 us
    all_gather x1 -> x0, waiting for transfers between devices: 34.4 us -> none  [per_device(): lax.all_gather(own_rows, 'blk', axis=0, tiled=True)]
    ppermute x0 -> x3, waiting for transfers between devices: none -> 17.9 us  [chains_change(): lax.ppermute(block_list[i0 - 1], ax_name, perm=[(hop_no, (hop_no - 1) % n...]
    unnamed x4 -> x13, local copies, waits for them, and re-layouts: 0.08 us -> 10.2 us
    ppermute x0 -> x3, starting transfers between devices: none -> 9.25 us  [chains_change(): lax.ppermute(block_list[i0 - 1], ax_name, perm=[(hop_no, (hop_no - 1) % n...]
    all_gather x1, blocking collectives: 12.8 us -> 16.3 us  [per_device(): lax.all_gather(own_weights, 'blk', axis=0, tiled=True)]
    dynamic_slice x0 -> x1, local copies, waits for them, and re-layouts: none -> 3.17 us  [chains_change(): jnp.roll(jnp.concatenate(block_list, axis=d_out), lax.axis_index(ax_name)...]
    concatenate x0 -> x1, local copies, waits for them, and re-layouts: none -> 1.9 us  [chains_change(): jnp.roll(jnp.concatenate(block_list, axis=d_out), lax.axis_index(ax_name)...]
  transfers between devices with their start and end apart: 2 -> 4, of which waited for: 2 -> 3; matrix products, arithmetic and copies ran while one was open for 3% -> 7% of each run, Pallas kernels for 0% -> 0%
where the time goes in v1:
time: 105 us
  waiting for transfers between devices  38.2 us (36%)
  local copies, waits for them, and re-layouts  22.3 us (21%)
  blocking collectives  16.3 us (16%)
  between operations  13.5 us (13%)
  starting transfers between devices  9.26 us (9%)
  matrix products  3.86 us (4%)
  other arithmetic  1.46 us (1%)
    reduce_scatter x1, waiting for transfers between devices, per_device(): lax.psum_scatter(products * picked_weights[:, None] * mask_rows, 'ckpt',...  20.3 us
    ppermute x3, waiting for transfers between devices, chains_change(): lax.ppermute(block_list[i0 - 1], ax_name, perm=[(hop_no, (hop_no - 1) % n...  17.9 us
    all_gather x1, blocking collectives, per_device(): lax.all_gather(own_weights, 'blk', axis=0, tiled=True)  16.3 us
    unnamed x13, local copies, waits for them, and re-layouts  10.2 us
    ppermute x3, starting transfers between devices, chains_change(): lax.ppermute(block_list[i0 - 1], ax_name, perm=[(hop_no, (hop_no - 1) % n...  9.25 us
    dot_general x1, matrix products, per_device(): lax.dot_general(picked, queries, (((1,), (1,)), ((), ())), preferred_elem...  3.86 us
    gather x1, local copies, waits for them, and re-layouts, per_device(): row_blocks[tile_owner]  3.62 us
    dynamic_slice x1, local copies, waits for them, and re-layouts, chains_change(): jnp.roll(jnp.concatenate(block_list, axis=d_out), lax.axis_index(ax_name)...  3.17 us
  transfers between devices with their start and end apart: 4, of which 3 were waited for; matrix products, arithmetic and copies ran while one was open for 7% of the time, Pallas kernels for 0%

profile of v1, /device:TPU:0, one launch (start us, length us, event | category | flops | bytes accessed | tf_op | source)
XLA Modules:
  0.0 104.8 jit_solution(15724882012996473232)
XLA Ops:
  6.5 0.0 copy-start
  6.5 0.0 copy-start.1
  6.5 0.0 reduce-scatter.2.cloned.1.call-start
  6.5 5.1 %collective-permute-start = (bf16[128,2048]{1,0:T(8,128)(2,1)}, bf16[128,2048]{1,0:T(8,128)(2,1)S(1)}, u32[]{:S(2)}, u32[]{:S(2)}) collective-permute-start(bf16[128,2048]{1,0:T(8,128)(2,1)} %bitcast.28), channel_id=1, source_target_pairs={{0,12},{4,0},{8,4},{12,8},{1,13},{5,1},{9,5},{13,9},{2,14},{6,2},{... | collective-permute-start | bytes 1572872 | tf_op jit(solution)/shard_map/ppermute | solution.py:16
  11.6 0.8 compare_reduce_fusion
  12.4 0.1 copy.7
  12.5 0.7 compare_select_fusion
  13.1 0.1 broadcast_bitcast_fusion
  13.2 9.9 %collective-permute-done = bf16[128,2048]{1,0:T(8,128)(2,1)S(1)} collective-permute-done((bf16[128,2048]{1,0:T(8,128)(2,1)}, bf16[128,2048]{1,0:T(8,128)(2,1)S(1)}, u32[]{:S(2)}, u32[]{:S(2)}) %collective-permute-start) | collective-permute-done | bytes 524320 | tf_op jit(solution)/shard_map/ppermute | solution.py:16
  23.1 4.2 %collective-permute-start.1 = (bf16[128,2048]{1,0:T(8,128)(2,1)S(1)}, bf16[128,2048]{1,0:T(8,128)(2,1)}, u32[]{:S(2)}, u32[]{:S(2)}) collective-permute-start(bf16[128,2048]{1,0:T(8,128)(2,1)S(1)} %collective-permute-done), channel_id=1, source_target_pairs={{0,12},{4,0},{8,4},{12,8},{1,13},{5,1},{9,5},{13,9},{2,14},{6,2},{... | collective-permute-start | bytes 1572872 | tf_op jit(solution)/shard_map/ppermute | solution.py:16
  27.3 16.3 %all-gather = bf16[1,512]{1,0:T(2,128)(2,1)S(1)} all-gather(bf16[1,128]{1,0:T(2,128)(2,1)} %param.7), channel_id=2, replica_groups=mesh['shard'=2,'blk'=4,'ckpt'=2,'qry'=2] {'blk'}, dimensions={1}, use_global_device_ids=true | all-gather | bytes 1280 | tf_op jit(solution)/shard_map/all_gather | solution.py:42
  43.6 0.6 gather_fusion.1
  44.2 1.9 %constant_dynamic-update-slice_fusion.7 = bf16[1024,2048]{1,0:T(8,128)(2,1)} fusion(bf16[1,128,2048]{2,1,0:T(8,128)(2,1)} %param.6), kind=kLoop, calls=%fused_computation.14 | loop fusion | bytes 1048576
  46.0 0.0 collective-permute-done.1
  46.0 0.0 collective-permute-start.2
  46.1 0.6 gather_fusion.2
  46.6 0.9 constant_dynamic-update-slice_fusion.6
  47.5 1.9 %constant_dynamic-update-slice_fusion.5 = bf16[1024,2048]{1,0:T(8,128)(2,1)} fusion(bf16[1024,2048]{1,0:T(8,128)(2,1)} %constant_dynamic-update-slice_fusion.6, bf16[128,2048]{1,0:T(8,128)(2,1)} %collective-permute-done.1), kind=kLoop, calls=%fused_computation.12 | loop fusion | bytes 1048576
  49.4 8.0 %collective-permute-done.2 = bf16[128,2048]{1,0:T(8,128)(2,1)} collective-permute-done((bf16[128,2048]{1,0:T(8,128)(2,1)}, bf16[128,2048]{1,0:T(8,128)(2,1)}, u32[]{:S(2)}, u32[]{:S(2)}) %collective-permute-start.2) | collective-permute-done | bytes 524320 | tf_op jit(solution)/shard_map/ppermute | solution.py:16
  57.4 1.9 %constant_dynamic-update-slice_fusion.4 = bf16[1024,2048]{1,0:T(8,128)(2,1)} fusion(bf16[1024,2048]{1,0:T(8,128)(2,1)} %constant_dynamic-update-slice_fusion.5, bf16[128,2048]{1,0:T(8,128)(2,1)} %collective-permute-done.2), kind=kLoop, calls=%fused_computation.11 | loop fusion | bytes 1048576
  59.3 0.0 copy-done.1
  59.3 0.8 constant_dynamic-update-slice_fusion.3
  60.2 0.9 constant_dynamic-update-slice_fusion.2
  61.0 1.9 %constant_dynamic-update-slice_fusion.1 = bf16[1024,2048]{1,0:T(8,128)(2,1)} fusion(bf16[1024,2048]{1,0:T(8,128)(2,1)} %constant_dynamic-update-slice_fusion.2, bf16[128,2048]{1,0:T(8,128)(2,1)} %collective-permute-done.1), kind=kLoop, calls=%fused_computation.8 | loop fusion | bytes 1048576
  62.9 1.9 %constant_dynamic-update-slice_fusion = bf16[1024,2048]{1,0:T(8,128)(2,1)} fusion(bf16[1024,2048]{1,0:T(8,128)(2,1)} %constant_dynamic-update-slice_fusion.1, bf16[128,2048]{1,0:T(8,128)(2,1)} %collective-permute-done.2), kind=kLoop, calls=%fused_computation.7 | loop fusion | bytes 1048576 | tf_op jit(solution)/shard_map/jit(_roll_dynamic)/concatenate | solution.py:22
  64.8 3.2 %constant_dynamic-slice_fusion = bf16[512,2048]{1,0:T(8,128)(2,1)} fusion(bf16[1024,2048]{1,0:T(8,128)(2,1)} %constant_dynamic-update-slice_fusion, s32[]{:T(128)S(6)} %select_n.19), kind=kLoop, calls=%fused_computation.20 | loop fusion | bytes 4194308 | tf_op jit(solution)/shard_map/jit(_roll_dynamic)/dynamic_slice | solution.py:22
  68.0 3.6 %gather_fusion = bf16[4,128,2048]{2,1,0:T(8,128)(2,1)} fusion(bf16[4,128,2048]{2,1,0:T(8,128)(2,1)} %bitcast.26, s32[1024]{0:T(1024)S(1)} %pad_clamp_fusion), kind=kCustom, calls=%fused_computation | custom fusion | bytes 4194320 | tf_op jit(solution)/shard_map/gather | solution.py:48
  71.6 0.1 broadcast_in_dim.16
  71.7 0.0 copy-done
  71.7 3.9 %fusion.5 = f32[512,512]{1,0:T(8,128)} fusion(f32[512,512]{1,0:T(8,128)S(1)} %bitcast.29, bf16[512,2048]{1,0:T(8,128)(2,1)} %bitcast.27, bf16[1,512,2048]{2,1,0:T(8,128)(2,1)S(1)} %copy-done, f32[512]{0:T(512)S(1)} %bitcast_convert_fusion), kind=kOutput, calls=%fused_computation.6 | convolution fusion | flops 1074266112 | bytes 6293504 | tf_op jit(solution)/shard_map/dot_general | solution.py:52
  75.6 0.0 reduce-scatter.2.cloned.1.call-update
  75.6 20.3 %reduce-scatter.2.cloned.1.call-done = f32[256,512]{1,0:T(8,128)} async-done(((f32[512,512]{1,0:T(8,128)}), f32[256,512]{1,0:T(8,128)}) %reduce-scatter.2.cloned.1.call-update) | async-done | bytes 524304 | tf_op jit(solution)/shard_map/reduce_scatter | solution.py:56
  95.9 2.0 %copy.8 = f32[512,256]{1,0:T(8,128)} copy(f32[512,256]{0,1:T(8,128)} %bitcast.31) | data formatting | bytes 1048576 | tf_op jit(solution)/shard_map/transpose | solution.py:59
  (5 shorter events, 0.0 us)
Async XLA Ops:
  6.5 65.2 %copy-start = (bf16[1,512,2048]{2,1,0:T(8,128)(2,1)S(1)}, bf16[1,512,2048]{2,1,0:T(8,128)(2,1)}, u32[]{:S(2)}) copy-start(bf16[1,512,2048]{2,1,0:T(8,128)(2,1)} %param.5) | copy-start | bytes 6291460
  6.5 52.8 %copy-start.1 = (bf16[1,128,2048]{2,1,0:T(8,128)(2,1)S(1)}, bf16[1,128,2048]{2,1,0:T(8,128)(2,1)}, u32[]{:S(2)}) copy-start(bf16[1,128,2048]{2,1,0:T(8,128)(2,1)} %param.6) | copy-start | bytes 1572868
  6.5 89.3 %reduce-scatter.2.cloned.1.call-start = ((), (), s32[]{:S(2)}) async-start(), calls=%async_computation.1 | async-start | bytes 1572864 | tf_op jit(solution)/shard_map/reduce_scatter | solution.py:56
  6.5 16.6 %collective-permute-start = (bf16[128,2048]{1,0:T(8,128)(2,1)}, bf16[128,2048]{1,0:T(8,128)(2,1)S(1)}, u32[]{:S(2)}, u32[]{:S(2)}) collective-permute-start(bf16[128,2048]{1,0:T(8,128)(2,1)} %bitcast.28), channel_id=1, source_target_pairs={{0,12},{4,0},{8,4},{12,8},{1,13},{5,1},{9,5},{13,9},{2,14},{6,2},{... | collective-permute-start | bytes 1572872 | tf_op jit(solution)/shard_map/ppermute | solution.py:16
  23.1 22.9 %collective-permute-start.1 = (bf16[128,2048]{1,0:T(8,128)(2,1)S(1)}, bf16[128,2048]{1,0:T(8,128)(2,1)}, u32[]{:S(2)}, u32[]{:S(2)}) collective-permute-start(bf16[128,2048]{1,0:T(8,128)(2,1)S(1)} %collective-permute-done), channel_id=1, source_target_pairs={{0,12},{4,0},{8,4},{12,8},{1,13},{5,1},{9,5},{13,9},{2,14},{6,2},{... | collective-permute-start | bytes 1572872 | tf_op jit(solution)/shard_map/ppermute | solution.py:16
  46.0 11.4 %collective-permute-start.2 = (bf16[128,2048]{1,0:T(8,128)(2,1)}, bf16[128,2048]{1,0:T(8,128)(2,1)}, u32[]{:S(2)}, u32[]{:S(2)}) collective-permute-start(bf16[128,2048]{1,0:T(8,128)(2,1)} %collective-permute-done.1), channel_id=1, source_target_pairs={{0,12},{4,0},{8,4},{12,8},{1,13},{5,1},{9,5},{13,9},{2,14},{6,2},{... | collective-permute-start | bytes 1572872 | tf_op jit(solution)/shard_map/ppermute | solution.py:16
Sparse Core Ops, SparseCore 0:
  75.7 20.0 reduce-scatter.1
